TPU v7x, 32 devices: a whole 2x2x4 slice. The times are simulated.
32 devices in a mesh: dp: 8 (over y, x, core), seq: 4 (over z).
Axes of the slice: x: 2, y: 2, z: 4, core: 2. Of those that a mesh axis runs over, the one named last changes fastest.
Arguments:
- video: bfloat16 [8, 512, 3072], P('dp', 'seq'), may hold values from -6 to 6
- cotangent: bfloat16 [8, 512, 3072], P('dp', 'seq'), may hold values from -6 to 6
- w_query: bfloat16 [3072, 3072], P(None, 'seq'), may hold values from -0.109375 to 0.109375
- w_out: bfloat16 [3072, 3072], P('seq'), may hold values from -0.109375 to 0.109375
- ref_kv: bfloat16 [8, 2, 1024, 3072], P('dp', None, 'seq'), may hold values from -400 to 400, as said below
- tile_lists: int32 [8, 2, 4, 3], P('dp'), may hold values from -1 to 3, as said below
Outputs:
- output: bfloat16 [8, 512, 3072], P('dp', 'seq')
- grad_video: bfloat16 [8, 512, 3072], P('dp', 'seq')
- grad_wq: float32 [3072, 3072], P(None, 'seq')
- grad_wo: float32 [3072, 3072], P('seq')
- grad_ref: bfloat16 [8, 2, 1024, 3072], P('dp', None, 'seq')
Inputs may be any that keep to these rules, and one draw needn't show every extreme that they name: `ref_kv`: values are of order one; key rows may carry scales of up to some tens. `tile_lists`: each row lists first 1 to 3 different tile indices from 0 to 3, consecutive modulo 4, then -1; the first video tile of every clip lists exactly 3 tiles for each person.
All inputs are finite; a program needn't handle non-finite values.
Results may differ from a plain program's by a relative error of at most 0.012.
The roundings to bfloat16 on the way count: a program that leaves them out, or rounds other values in their place, can miss the bound.
Values may be sent and summed in bfloat16 or wider, within the bound.
No kernel may reach another device: no remote copies, remote signals or barrier semaphores. Data moves between devices by JAX's collectives and lax.ppermute only.
A program may use at most 128 MiB of HBM per device.

v0:
```python
import math
import jax
import jax.numpy as jnp
from jax import lax
from jax.sharding import PartitionSpec as P

HD = 128
REF = 512
TILE = 128


def build_allowed(tile_lists, tile_size, ref_tokens):
    tiles_each = ref_tokens // tile_size
    matched = jnp.any(tile_lists[..., None] == jnp.arange(tiles_each, dtype=jnp.int32), axis=-2)
    tile_table = jnp.transpose(matched, (1, 0, 2)).reshape(matched.shape[1], -1)
    return jnp.repeat(jnp.repeat(tile_table, tile_size, axis=0), tile_size, axis=1)


def split_heads(array, heads_count):
    return jnp.transpose(array.reshape(array.shape[0], heads_count, -1), (1, 0, 2))


def merge_heads(array):
    return jnp.transpose(array, (1, 0, 2)).reshape(array.shape[1], -1)


def contract_last(left, right):
    return lax.dot_general(
        left, right, (((1,), (1,)), ((), ())), preferred_element_type=jnp.float32
    )


def contract_first(left, right):
    return lax.dot_general(
        left, right, (((0,), (0,)), ((), ())), preferred_element_type=jnp.float32
    )


def softmax_weights(query, keys, allowed, score_scale):
    scores = contract_last(query, keys) * score_scale
    scores = jnp.where(allowed, scores, -1e30)
    peak = jnp.max(scores, axis=-1, keepdims=True)
    weights = jnp.exp(scores - peak)
    return weights / jnp.sum(weights, axis=-1, keepdims=True)


def head_forward(query, keys, values, allowed, score_scale):
    weights = softmax_weights(query, keys, allowed, score_scale)
    probs = weights.astype(jnp.bfloat16)
    return jnp.dot(probs, values, preferred_element_type=jnp.float32).astype(jnp.bfloat16)


def head_backward(query, keys, values, grad_out, allowed, score_scale):
    weights = softmax_weights(query, keys, allowed, score_scale)
    probs = weights.astype(jnp.bfloat16)
    grad_probs = contract_last(grad_out, values)
    delta = jnp.sum(grad_probs * weights, axis=-1, keepdims=True)
    grad_scores = (weights * (grad_probs - delta) * score_scale).astype(jnp.bfloat16)
    grad_query = jnp.dot(grad_scores, keys, preferred_element_type=jnp.float32).astype(jnp.bfloat16)
    grad_keys = contract_first(grad_scores, query).astype(jnp.bfloat16)
    grad_values = contract_first(probs, grad_out).astype(jnp.bfloat16)
    return (grad_query, grad_keys, grad_values)


def body(video, cotangent, w_query, w_out, ref_kv, tile_lists):
    local_width = w_query.shape[1]
    heads_here = local_width // HD
    score_scale = 1.0 / math.sqrt(HD)
    gathered = lax.all_gather(video, "seq", axis=1, tiled=True)[0]
    query = jnp.dot(gathered, w_query, preferred_element_type=jnp.float32).astype(jnp.bfloat16)
    both_kv = lax.all_to_all(ref_kv, "seq", split_axis=3, concat_axis=2, tiled=True)[0]
    allowed = build_allowed(tile_lists[0], TILE, REF)
    q_heads = split_heads(query, heads_here)
    k_heads = split_heads(both_kv[0], heads_here)
    v_heads = split_heads(both_kv[1], heads_here)
    attn_heads = lax.map(
        lambda item: head_forward(item[0], item[1], item[2], allowed, score_scale),
        (q_heads, k_heads, v_heads),
    )
    attention = merge_heads(attn_heads)
    rows = attention
    output = lax.psum_scatter(
        jnp.dot(rows, w_out, preferred_element_type=jnp.float32),
        "seq",
        scatter_dimension=0,
        tiled=True,
    )
    output = output.astype(jnp.bfloat16)[None]
    grad_rows = lax.all_gather(cotangent, "seq", axis=1, tiled=True)[0]
    grad_attention = contract_last(grad_rows, w_out).astype(jnp.bfloat16)
    grad_wo = contract_first(attention, grad_rows)
    back = lax.map(
        lambda item: head_backward(item[0], item[1], item[2], item[3], allowed, score_scale),
        (q_heads, k_heads, v_heads, split_heads(grad_attention, heads_here)),
    )
    grad_query = merge_heads(back[0])
    grad_kv = jnp.stack([merge_heads(back[1]), merge_heads(back[2])])[None]
    grad_ref = lax.all_to_all(grad_kv, "seq", split_axis=2, concat_axis=3, tiled=True)
    rows = grad_query
    grad_video = lax.psum_scatter(
        contract_last(rows, w_query).astype(jnp.bfloat16), "seq", scatter_dimension=0, tiled=True
    ).astype(jnp.float32)
    grad_video = grad_video.astype(jnp.bfloat16)[None]
    grad_wq = contract_first(gathered, grad_query)
    grad_wq, grad_wo = (
        lax.psum(grad_wq.astype(jnp.bfloat16), "dp").astype(jnp.float32),
        lax.psum(grad_wo.astype(jnp.bfloat16), "dp").astype(jnp.float32),
    )
    return (output, grad_video, grad_wq, grad_wo, grad_ref)


def solution(mesh):
    in_specs = (
        P("dp", "seq", None),
        P("dp", "seq", None),
        P(None, "seq"),
        P("seq", None),
        P("dp", None, "seq", None),
        P("dp", None, None, None),
    )
    out_specs = (
        P("dp", "seq", None),
        P("dp", "seq", None),
        P(None, "seq"),
        P("seq", None),
        P("dp", None, "seq", None),
    )
    return jax.shard_map(body, mesh=mesh, in_specs=in_specs, out_specs=out_specs, check_vma=False)
```

profile of v0, /device:TPU:0, one launch (start us, length us, event | category | flops | bytes accessed | tf_op | source)
XLA Modules:
  0.0 661.5 jit_solution(8851351125706962845)
XLA Ops:
  8.6 8.6 %copy.77 = bf16[1,2,256,3072]{2,1,0,3:T(2,128)(2,1)} copy(bf16[1,2,256,3072]{3,2,1,0:T(8,128)(2,1)} %param.14) | data formatting | bytes 6291456 | tf_op args[4]
  17.3 6.4 all-to-all-start
  24.1 109.5 %all-gather.5.cloned.1.call-done = bf16[1,512,3072]{2,1,0:T(8,128)(2,1)} async-done(((bf16[1,128,3072]{2,1,0:T(8,128)(2,1)}), bf16[1,512,3072]{2,1,0:T(8,128)(2,1)}) %all-gather.5.cloned.1.call-update) | async-done | bytes 3145744 | tf_op jit(solution)/shard_map/all_gather | solution.py:89
  133.5 6.8 %fusion.51 = bf16[512,768]{1,0:T(8,128)(2,1)} fusion(bf16[768,3072]{1,0:T(8,128)(2,1)} %param.13, bf16[1,512,3072]{2,1,0:T(8,128)(2,1)} %all-gather.5.cloned.1.call-done), kind=kOutput, calls=%fused_computation.66 | convolution fusion | flops 2416312320 | bytes 8650752 | tf_op jit(solution)/shard_map/dot_general | solution.py:28
  140.4 2.4 copy.86
  142.7 54.0 %all-gather.3.cloned.1.call-done = bf16[1,512,3072]{2,1,0:T(8,128)(2,1)} async-done(((bf16[1,128,3072]{2,1,0:T(8,128)(2,1)}), bf16[1,512,3072]{2,1,0:T(8,128)(2,1)}) %all-gather.3.cloned.1.call-update) | async-done | bytes 3145744 | tf_op jit(solution)/shard_map/all_gather | solution.py:69
  196.7 6.8 %fusion.48 = bf16[512,768]{1,0:T(8,128)(2,1)} fusion(bf16[3072,768]{1,0:T(8,128)(2,1)} %param.12, bf16[1,512,3072]{2,1,0:T(8,128)(2,1)} %all-gather.3.cloned.1.call-done), kind=kOutput, calls=%fused_computation.65 | convolution fusion | flops 2416312320 | bytes 8650752 | tf_op jit(solution)/shard_map/dot_general | solution.py:70
  203.5 2.3 copy.76
  205.8 2.3 copy.82
  208.1 2.4 copy.113
  210.5 2.2 fusion.57
  212.7 2.8 reshape_squeeze.7
  219.9 32.9 %while.26 = (s32[]{:T(128)}, bf16[6,512,128]{1,2,0:T(8,128)(2,1)S(1)}, bf16[6,512,128]{2,1,0:T(8,128)(2,1)}, bf16[6,1024,128]{2,1,0:T(8,128)(2,1)}, bf16[6,1024,...) while((s32[]{:T(128)}, bf16[6,512,128]{1,2,0:T(8,128)(2,1)S(1)}, ...), condition=%wide.region_4.5_spmd.clone, body=%wide.region_1.4_spmd.clone.sunk | while | flops 272694272 | bytes 8666205 | solution.py:76
  219.9 1.6 broadcast_in_dim.65
  221.5 1.7 fusion.85
  225.4 1.6 broadcast_in_dim.65
  227.0 1.7 fusion.85
  230.9 1.6 broadcast_in_dim.65
  232.5 1.7 fusion.85
  236.4 1.6 broadcast_in_dim.65
  238.0 1.7 fusion.85
  241.9 1.6 broadcast_in_dim.65
  243.5 1.7 fusion.85
  247.3 1.6 broadcast_in_dim.65
  249.0 1.7 fusion.85
  253.8 76.0 %while.27 = (s32[]{:T(128)}, bf16[6,512,128]{1,2,0:T(8,128)(2,1)}, bf16[6,1024,128]{1,2,0:T(8,128)(2,1)}, bf16[6,1024,128]{1,2,0:T(8,128)(2,1)}, bf16[6,512,128]...) while((s32[]{:T(128)}, bf16[6,512,128]{1,2,0:T(8,128)(2,1)}, ...), condition=%wide.region_10.11_spmd.clone, body=%wide.region_6.10_spmd.clone.sunk | while | flops 680851968 | bytes 23490688 | solution.py:92
  253.8 1.6 broadcast_in_dim.66
  255.4 1.7 fusion.94
  257.5 1.6 fusion.97
  259.3 1.8 multiply_reduce_fusion.2
  266.5 1.6 broadcast_in_dim.66
  268.1 1.7 fusion.94
  270.2 1.6 fusion.97
  272.0 1.8 multiply_reduce_fusion.2
  279.1 1.6 broadcast_in_dim.66
  280.7 1.7 fusion.94
  282.9 1.6 fusion.97
  284.7 1.8 multiply_reduce_fusion.2
  291.8 1.6 broadcast_in_dim.66
  293.4 1.7 fusion.94
  295.6 1.7 fusion.97
  297.4 1.8 multiply_reduce_fusion.2
  304.5 1.6 broadcast_in_dim.66
  306.1 1.7 fusion.94
  308.2 1.7 fusion.97
  310.0 1.8 multiply_reduce_fusion.2
  318.7 1.7 fusion.94
  320.9 1.6 fusion.97
  322.7 1.8 multiply_reduce_fusion.2
  329.8 7.1 %fusion.41 = bf16[3072,768]{0,1:T(8,128)(2,1)} fusion(bf16[512,768]{0,1:T(8,128)(2,1)} %bitcast.173, bf16[1,512,3072]{2,1,0:T(8,128)(2,1)} %all-gather.3.cloned.1.call-done), kind=kOutput, calls=%fused_computation.55 | convolution fusion | flops 2418278400 | bytes 8650752 | tf_op jit(solution)/shard_map/dot_general | solution.py:34
  336.9 4.2 convolution_convert_fusion.4
  341.2 7.1 %fusion.58 = f32[512,3072]{1,0:T(8,128)} fusion(bf16[512,768]{0,1:T(8,128)(2,1)S(1)} %bitcast.168, bf16[768,3072]{1,0:T(8,128)(2,1)} %param.13), kind=kOutput, calls=%fused_computation.73 | convolution fusion | flops 2415919104 | bytes 11796480 | tf_op jit(solution)/shard_map/dot_general | solution.py:83
  349.4 6.5 convolution_convert_fusion.6
  356.0 2.3 maximum_bitcast_fusion
  358.3 5.6 copy.94
  363.9 74.7 %all_to_all.33 = bf16[1,2,1024,768]{3,1,0,2:T(2,128)(2,1)S(1)} all-to-all(bf16[1,2,1024,768]{3,1,0,2:T(2,128)(2,1)} %copy.94), channel_id=1, replica_groups=mesh['dp'=8,'seq'=4] {'seq'}, dimensions={2} | all-to-all | bytes 6291456 | tf_op jit(solution)/shard_map/all_to_all | solution.py:98
  439.1 2.8 copy.96
  441.9 4.7 copy.98
  446.6 31.6 %all-reduce.3.cloned.1.call-done = (bf16[3072,768]{0,1:T(8,128)(2,1)}, bf16[768,3072]{1,0:T(8,128)(2,1)}) async-done(((bf16[3072,768]{0,1:T(8,128)(2,1)}, bf16[768,3072]{1,0:T(8,128)(2,1)}), (bf16[3072,768]{0,1:T(8,128)(2,1)}, bf16[768,3072]{1,0:T(8,128)(2,1)})) %all-reduce.3.cloned.1.call-update) | async-done | bytes 9437200 | tf_op jit(solution)/shard_map/psum | solution.py:106
  478.2 7.4 %copy.97 = f32[3072,768]{1,0:T(8,128)} copy(bf16[3072,768]{0,1:T(8,128)(2,1)} %get-tuple-element.241) | data formatting | bytes 14155776
  485.6 8.5 %convert_element_type.58 = f32[768,3072]{1,0:T(8,128)} convert(bf16[768,3072]{1,0:T(8,128)(2,1)} %get-tuple-element.242) | non-fusion elementwise | flops 2359296 | bytes 14155776 | tf_op jit(solution)/shard_map/convert_element_type | solution.py:107
  494.1 97.3 %reduce-scatter.3.cloned.1.call-done = f32[128,3072]{1,0:T(8,128)} async-done(((f32[512,3072]{1,0:T(8,128)}), f32[128,3072]{1,0:T(8,128)}) %reduce-scatter.3.cloned.1.call-update) | async-done | bytes 1572880 | tf_op jit(solution)/shard_map/reduce_scatter | solution.py:82
  591.3 2.4 convert_bitcast_fusion
  593.7 61.3 %reduce-scatter.5.cloned.1.call-done = bf16[128,3072]{1,0:T(8,128)(2,1)} async-done(((bf16[512,3072]{1,0:T(8,128)(2,1)}), bf16[128,3072]{1,0:T(8,128)(2,1)}) %reduce-scatter.5.cloned.1.call-update) | async-done | bytes 786448 | tf_op jit(solution)/shard_map/reduce_scatter | solution.py:100
  (109 shorter events, 58.2 us)
Async XLA Ops:
  7.2 126.4 %all-gather.5.cloned.1.call-start = ((), (), s32[]{:S(2)}) async-start(), calls=%async_computation.6 | async-start | bytes 3932160 | tf_op jit(solution)/shard_map/all_gather | solution.py:89
  7.9 188.8 %all-gather.3.cloned.1.call-start = ((), (), s32[]{:S(2)}) async-start(), calls=%async_computation.4 | async-start | bytes 3932160 | tf_op jit(solution)/shard_map/all_gather | solution.py:69
  17.3 6.5 copy-start.1
  17.3 190.8 %all-to-all-start = ((bf16[1,2,256,3072]{2,1,0,3:T(2,128)(2,1)}), bf16[1,2,256,3072]{2,1,0,3:T(2,128)(2,1)S(1)}, u32[]{:S(2)}, u32[]{:S(2)}) async-start(bf16[1,2,256,3072]{2,1,0,3:T(2,128)(2,1)} %copy.77), calls=%async_computation | async-start | bytes 6291456 | tf_op jit(solution)/shard_map/all_to_all | solution.py:71
  23.7 454.5 %all-reduce.3.cloned.1.call-start = ((), (), s32[]{:S(2)}) async-start(), calls=%async_computation.8 | async-start | bytes 18874368 | tf_op jit(solution)/shard_map/psum | solution.py:106
  329.8 7.1 %copy-start.2 = (bf16[1,512,3072]{2,1,0:T(8,128)(2,1)S(1)}, bf16[1,512,3072]{2,1,0:T(8,128)(2,1)}, u32[]{:S(2)}) copy-start(bf16[1,512,3072]{2,1,0:T(8,128)(2,1)} %all-gather.5.cloned.1.call-done) | copy-start | bytes 9437188
  341.1 250.2 %reduce-scatter.3.cloned.1.call-start = ((), (), s32[]{:S(2)}) async-start(), calls=%async_computation.5 | async-start | bytes 7864320 | tf_op jit(solution)/shard_map/reduce_scatter | solution.py:82
  348.3 1.1 copy-start
  348.3 306.6 %reduce-scatter.5.cloned.1.call-start = ((), (), s32[]{:S(2)}) async-start(), calls=%async_computation.7 | async-start | bytes 3932160 | tf_op jit(solution)/shard_map/reduce_scatter | solution.py:100
Sparse Core Ops, SparseCore 0:
  9.6 123.9 all-gather.4
  135.1 61.5 all-gather.2
  341.3 136.9 all-reduce.2
  480.5 110.8 reduce-scatter.2
  594.2 60.7 reduce-scatter.4
where the time goes:
time: 664 us; the launch traced here: 662 us
  waiting for transfers between devices  355 us (53%)
  matrix products  106 us (16%)
  local copies, waits for them, and re-layouts  82 us (12%)
  blocking collectives  74.7 us (11%)
  other arithmetic  23.1 us (3%)
  between operations  13.8 us (2%)
    all_gather x1, waiting for transfers between devices, body(): grad_rows = lax.all_gather(cotangent, 'seq', axis=1, tiled=True)[0]  109 us
    reduce_scatter x1, waiting for transfers between devices, body(): lax.psum_scatter(jnp.dot(rows, w_out, preferred_element_type=jnp.float32)...  97.3 us
    all_to_all x1, blocking collectives, body(): lax.all_to_all(grad_kv, 'seq', split_axis=2, concat_axis=3, tiled=True)  74.7 us
    reduce_scatter x1, waiting for transfers between devices, body(): lax.psum_scatter(contract_last(rows, w_query).astype(jnp.bfloat16), 'seq'...  61.3 us
    all_gather x1, waiting for transfers between devices, body(): gathered = lax.all_gather(video, 'seq', axis=1, tiled=True)[0]  54 us
    dot_general x20, matrix products, contract_last(): lax.dot_general(left, right, (((1,), (1,)), ((), ())), preferred_element_...  44.7 us
    psum x1, waiting for transfers between devices, body(): lax.psum(grad_wq.astype(jnp.bfloat16), 'dp').astype(jnp.float32)  31.6 us
    dot_general x14, matrix products, contract_first(): lax.dot_general(left, right, (((0,), (0,)), ((), ())), preferred_element_...  29.6 us
  transfers between devices with their start and end apart: 6, of which 5 were waited for; matrix products, arithmetic and copies ran while one was open for 12% of the time, Pallas kernels for 0%

commit v1 on v0

--- a/solution.py
+++ b/solution.py
@@ -7,6 +7,23 @@
 HD = 128
 REF = 512
 TILE = 128
+
+
+def pair_cycles(field_in, in_dim):
+    t1 = list(field_in.shape[1:])
+    t1[in_dim] *= field_in.shape[0]
+    return jnp.moveaxis(field_in, 0, in_dim).reshape(t1)
+
+
+def write_desk(local, shard_axis):
+    w2, spare = (jax.lax.axis_size(shard_axis), jax.lax.axis_index(shard_axis))
+    tmp, found_now = (local[None], 1)
+    while found_now < w2:
+        t_next = jax.lax.ppermute(tmp, shard_axis, [(d, d ^ found_now) for d in range(w2)])
+        u_next = spare & found_now == 0
+        tmp = jnp.concatenate([jnp.where(u_next, tmp, t_next), jnp.where(u_next, t_next, tmp)])
+        found_now *= 2
+    return tmp
 
 
 def build_allowed(tile_lists, tile_size, ref_tokens):
@@ -86,7 +103,11 @@
         tiled=True,
     )
     output = output.astype(jnp.bfloat16)[None]
-    grad_rows = lax.all_gather(cotangent, "seq", axis=1, tiled=True)[0]
+
+    def answer_marks_by_axis(v0, unit, along_dim):
+        return pair_cycles(write_desk(v0, unit), along_dim)
+
+    grad_rows = answer_marks_by_axis(cotangent, "seq", along_dim=1)[0]
     grad_attention = contract_last(grad_rows, w_out).astype(jnp.bfloat16)
     grad_wo = contract_first(attention, grad_rows)
     back = lax.map(

time: 664 us -> 689 us (1.038)
  waiting for transfers between devices: 355 us -> 372 us
    ppermute x0 -> x2, waiting for transfers between devices: none -> 181 us  [write_desk(): jax.lax.ppermute(tmp, shard_axis, [(d, d ^ found_now) for d in range(w2)])]
    all_gather x1 -> x0, waiting for transfers between devices: 109 us -> none  [body(): grad_rows = lax.all_gather(cotangent, 'seq', axis=1, tiled=True)[0]]
    all_gather x1, waiting for transfers between devices: 54 us -> 0.01 us  [body(): gathered = lax.all_gather(video, 'seq', axis=1, tiled=True)[0]]
    unnamed x12 -> x22, local copies, waits for them, and re-layouts: 27.2 us -> 29 us
  transfers between devices with their start and end apart: 6 -> 7, of which waited for: 5 -> 5; matrix products, arithmetic and copies ran while one was open for 12% -> 12% of each run, Pallas kernels for 0% -> 0%
where the time goes in v1:
time: 689 us; the launch traced here: 687 us
  waiting for transfers between devices  372 us (54%)
  matrix products  104 us (15%)
  local copies, waits for them, and re-layouts  83.8 us (12%)
  blocking collectives  74.7 us (11%)
  other arithmetic  28.2 us (4%)
  between operations  13.9 us (2%)
  starting transfers between devices  8.87 us (1%)
    ppermute x2, waiting for transfers between devices, write_desk(): jax.lax.ppermute(tmp, shard_axis, [(d, d ^ found_now) for d in range(w2)])  181 us
    reduce_scatter x1, waiting for transfers between devices, body(): lax.psum_scatter(jnp.dot(rows, w_out, preferred_element_type=jnp.float32)...  97.4 us
    all_to_all x1, blocking collectives, body(): lax.all_to_all(grad_kv, 'seq', split_axis=2, concat_axis=3, tiled=True)  74.7 us
    reduce_scatter x1, waiting for transfers between devices, body(): lax.psum_scatter(contract_last(rows, w_query).astype(jnp.bfloat16), 'seq'...  61.3 us
    dot_general x20, matrix products, contract_last(): lax.dot_general(left, right, (((1,), (1,)), ((), ())), preferred_element_...  43.1 us
    psum x1, waiting for transfers between devices, body(): lax.psum(grad_wq.astype(jnp.bfloat16), 'dp').astype(jnp.float32)  32.3 us
    dot_general x14, matrix products, contract_first(): lax.dot_general(left, right, (((0,), (0,)), ((), ())), preferred_element_...  30.3 us
    unnamed x22, local copies, waits for them, and re-layouts  29 us
  transfers between devices with their start and end apart: 7, of which 5 were waited for; matrix products, arithmetic and copies ran while one was open for 12% of the time, Pallas kernels for 0%

profile of v1, /device:TPU:0, one launch (start us, length us, event | category | flops | bytes accessed | tf_op | source)
XLA Modules:
  0.0 686.8 jit_solution(709470550394449186)
XLA Ops:
  7.2 3.1 collective-permute-start
  10.3 8.6 %copy.77 = bf16[1,2,256,3072]{2,1,0,3:T(2,128)(2,1)} copy(bf16[1,2,256,3072]{3,2,1,0:T(8,128)(2,1)} %param.14) | data formatting | bytes 6291456 | tf_op args[4]
  19.0 3.9 all-to-all-start
  22.9 22.4 %collective-permute-done = bf16[1,1,128,3072]{3,2,1,0:T(8,128)(2,1)} collective-permute-done((bf16[1,1,128,3072]{3,2,1,0:T(8,128)(2,1)}, bf16[1,1,128,3072]{3,2,1,0:T(8,128)(2,1)}, u32[]{:S(2)}, u32[]{:S(2)}) %collective-permute-start) | collective-permute-done | bytes 786464 | tf_op jit(solution)/shard_map/ppermute | solution.py:22
  48.9 1.8 collective-permute-start.1
  51.0 158.9 %collective-permute-done.1 = bf16[2,1,128,3072]{3,2,1,0:T(8,128)(2,1)} collective-permute-done((bf16[2,1,128,3072]{3,2,1,0:T(8,128)(2,1)}, bf16[2,1,128,3072]{3,2,1,0:T(8,128)(2,1)}, u32[]{:S(2)}, u32[]{:S(2)}) %collective-permute-start.1) | collective-permute-done | bytes 1572896 | tf_op jit(solution)/shard_map/ppermute | solution.py:22
  209.9 2.0 broadcast_select_fusion.1
  212.2 1.7 copy-done.4
  213.9 5.9 convolution_convert_fusion.7
  219.8 2.3 copy.86
  222.1 6.8 fusion.45
  228.9 2.3 copy.76
  231.2 2.3 copy.82
  233.4 2.4 copy.113
  235.9 2.2 fusion.51
  238.1 2.8 reshape_squeeze.7
  244.6 32.2 %while.26 = (s32[]{:T(128)}, bf16[6,512,128]{1,2,0:T(8,128)(2,1)S(1)}, bf16[6,512,128]{2,1,0:T(8,128)(2,1)}, bf16[6,1024,128]{2,1,0:T(8,128)(2,1)S(1)}, bf16[6,1...) while((s32[]{:T(128)}, bf16[6,512,128]{1,2,0:T(8,128)(2,1)S(1)}, ...), condition=%wide.region_4.5_spmd.clone, body=%wide.region_1.4_spmd.clone.sunk | while | flops 272694272 | bytes 8666205 | solution.py:93
  244.6 1.6 broadcast_in_dim.69
  250.0 1.6 broadcast_in_dim.69
  251.6 1.6 fusion.81
  255.4 1.6 broadcast_in_dim.69
  260.7 1.6 broadcast_in_dim.69
  266.1 1.6 broadcast_in_dim.69
  271.5 1.6 broadcast_in_dim.69
  278.0 76.8 %while.27 = (s32[]{:T(128)}, bf16[6,512,128]{1,2,0:T(8,128)(2,1)}, bf16[6,1024,128]{1,2,0:T(8,128)(2,1)}, bf16[6,1024,128]{1,2,0:T(8,128)(2,1)}, bf16[6,512,128]...) while((s32[]{:T(128)}, bf16[6,512,128]{1,2,0:T(8,128)(2,1)}, ...), condition=%wide.region_10.11_spmd.clone, body=%wide.region_6.10_spmd.clone.sunk | while | flops 680851968 | bytes 36073656 | solution.py:113
  278.0 1.6 broadcast_in_dim.70
  279.6 1.7 fusion.90
  281.7 1.7 fusion.93
  283.5 1.8 multiply_reduce_fusion.2
  290.8 1.6 broadcast_in_dim.70
  292.4 1.7 fusion.90
  294.5 1.6 fusion.93
  296.3 1.8 multiply_reduce_fusion.2
  303.6 1.6 broadcast_in_dim.70
  305.2 1.7 fusion.90
  307.3 1.7 fusion.93
  309.1 1.8 multiply_reduce_fusion.2
  316.3 1.6 broadcast_in_dim.70
  317.9 1.7 fusion.90
  320.1 1.6 fusion.93
  321.9 1.8 multiply_reduce_fusion.2
  329.2 1.6 broadcast_in_dim.70
  330.8 1.7 fusion.90
  332.9 1.6 fusion.93
  334.7 1.8 multiply_reduce_fusion.2
  342.0 1.6 broadcast_in_dim.70
  343.6 1.7 fusion.90
  345.7 1.7 fusion.93
  347.5 1.8 multiply_reduce_fusion.2
  354.8 7.1 %convolution_convert_fusion.4 = bf16[768,3072]{1,0:T(8,128)(2,1)} fusion(bf16[512,768]{0,1:T(8,128)(2,1)} %bitcast.168, bf16[512,3072]{1,0:T(8,128)(2,1)} %bitcast.167), kind=kOutput, calls=%fused_computation.53 | convolution fusion | flops 2418278400 | bytes 8650752 | tf_op jit(solution)/shard_map/dot_general | solution.py:51
  361.8 4.2 fusion.41
  367.2 6.9 %fusion.52 = f32[512,3072]{1,0:T(8,128)} fusion(bf16[512,768]{0,1:T(8,128)(2,1)S(1)} %bitcast.169, bf16[768,3072]{1,0:T(8,128)(2,1)} %param.13), kind=kOutput, calls=%fused_computation.76 | convolution fusion | flops 2415919104 | bytes 11796480 | tf_op jit(solution)/shard_map/dot_general | solution.py:100
  374.2 6.5 convolution_convert_fusion.6
  380.7 2.2 maximum_bitcast_fusion
  382.9 5.6 copy.94
  388.6 74.7 %all_to_all.33 = bf16[1,2,1024,768]{3,1,0,2:T(2,128)(2,1)S(1)} all-to-all(bf16[1,2,1024,768]{3,1,0,2:T(2,128)(2,1)} %copy.94), channel_id=1, replica_groups=mesh['dp'=8,'seq'=4] {'seq'}, dimensions={2} | all-to-all | bytes 6291456 | tf_op jit(solution)/shard_map/all_to_all | solution.py:119
  463.7 2.8 copy.96
  466.5 4.6 copy.98
  471.1 32.3 %all-reduce.3.cloned.1.call-done = (bf16[3072,768]{0,1:T(8,128)(2,1)}, bf16[768,3072]{1,0:T(8,128)(2,1)}) async-done(((bf16[3072,768]{0,1:T(8,128)(2,1)}, bf16[768,3072]{1,0:T(8,128)(2,1)}), (bf16[3072,768]{0,1:T(8,128)(2,1)}, bf16[768,3072]{1,0:T(8,128)(2,1)})) %all-reduce.3.cloned.1.call-update) | async-done | bytes 9437200 | tf_op jit(solution)/shard_map/psum | solution.py:127
  503.4 7.4 %copy.97 = f32[3072,768]{1,0:T(8,128)} copy(bf16[3072,768]{0,1:T(8,128)(2,1)} %get-tuple-element.241) | data formatting | bytes 14155776
  510.8 8.5 %convert_element_type.58 = f32[768,3072]{1,0:T(8,128)} convert(bf16[768,3072]{1,0:T(8,128)(2,1)} %get-tuple-element.242) | non-fusion elementwise | flops 2359296 | bytes 14155776 | tf_op jit(solution)/shard_map/convert_element_type | solution.py:128
  519.3 97.4 %reduce-scatter.3.cloned.1.call-done = f32[128,3072]{1,0:T(8,128)} async-done(((f32[512,3072]{1,0:T(8,128)}), f32[128,3072]{1,0:T(8,128)}) %reduce-scatter.3.cloned.1.call-update) | async-done | bytes 1572880 | tf_op jit(solution)/shard_map/reduce_scatter | solution.py:99
  616.6 2.4 convert_bitcast_fusion
  619.0 61.3 %reduce-scatter.5.cloned.1.call-done = bf16[128,3072]{1,0:T(8,128)(2,1)} async-done(((bf16[512,3072]{1,0:T(8,128)(2,1)}), bf16[128,3072]{1,0:T(8,128)(2,1)}) %reduce-scatter.5.cloned.1.call-update) | async-done | bytes 786448 | tf_op jit(solution)/shard_map/reduce_scatter | solution.py:121
  (148 shorter events, 67.1 us)
Async XLA Ops:
  7.2 214.9 %all-gather.2.cloned.1.call-start = ((), (), s32[]{:S(2)}) async-start(), calls=%async_computation.4 | async-start | bytes 3932160 | tf_op jit(solution)/shard_map/all_gather | solution.py:86
  7.2 38.0 %collective-permute-start = (bf16[1,1,128,3072]{3,2,1,0:T(8,128)(2,1)}, bf16[1,1,128,3072]{3,2,1,0:T(8,128)(2,1)}, u32[]{:S(2)}, u32[]{:S(2)}) collective-permute-start(bf16[1,1,128,3072]{3,2,1,0:T(8,128)(2,1)} %bitcast.176), channel_id=1, source_target_pairs={{0,1},{1,0},{2,3},{3,2},{4,5},{5,4},{6,7},{7,6},{8,9},{9,8},{10,11... | collective-permute-start | bytes 2359304 | tf_op jit(solution)/shard_map/ppermute | solution.py:22
  19.0 214.5 %all-to-all-start = ((bf16[1,2,256,3072]{2,1,0,3:T(2,128)(2,1)}), bf16[1,2,256,3072]{2,1,0,3:T(2,128)(2,1)S(1)}, u32[]{:S(2)}, u32[]{:S(2)}) async-start(bf16[1,2,256,3072]{2,1,0,3:T(2,128)(2,1)} %copy.77), calls=%async_computation | async-start | bytes 6291456 | tf_op jit(solution)/shard_map/all_to_all | solution.py:88
  22.8 480.5 %all-reduce.3.cloned.1.call-start = ((), (), s32[]{:S(2)}) async-start(), calls=%async_computation.7 | async-start | bytes 18874368 | tf_op jit(solution)/shard_map/psum | solution.py:127
  46.7 0.9 copy-start
  46.7 2.2 copy-start.1
  46.7 3.9 copy-start.8
  48.9 161.0 %collective-permute-start.1 = (bf16[2,1,128,3072]{3,2,1,0:T(8,128)(2,1)}, bf16[2,1,128,3072]{3,2,1,0:T(8,128)(2,1)}, u32[]{:S(2)}, u32[]{:S(2)}) collective-permute-start(bf16[2,1,128,3072]{3,2,1,0:T(8,128)(2,1)} %pad_maximum_fusion.1), channel_id=1, source_target_pairs={{0,2},{1,3},{2,0},{3,1},{4,6},{5,7},{6,4},{7,5},{8,10},{9,11},{10,... | collective-permute-start | bytes 4718600 | tf_op jit(solution)/shard_map/ppermute | solution.py:22
  212.2 1.7 copy-start.4
  276.8 1.1 copy-start.5
  278.0 1.6 copy-start.2
  287.5 3.3 copy-start.3
  290.8 1.6 copy-start.2
  300.3 3.3 copy-start.3
  303.5 1.6 copy-start.2
  313.0 3.3 copy-start.3
  316.3 1.6 copy-start.2
  325.8 3.3 copy-start.3
  329.2 1.6 copy-start.2
  338.6 3.3 copy-start.3
  342.0 1.6 copy-start.2
  351.5 3.3 copy-start.3
  354.8 7.1 %copy-start.7 = (bf16[6,512,128]{1,2,0:T(8,128)(2,1)S(1)}, bf16[6,512,128]{1,2,0:T(8,128)(2,1)}, u32[]{:S(2)}) copy-start(bf16[6,512,128]{1,2,0:T(8,128)(2,1)} %get-tuple-element.87) | copy-start | bytes 2359300
  354.8 7.1 %copy-start.9 = (bf16[1,512,3072]{2,1,0:T(8,128)(2,1)S(1)}, bf16[1,512,3072]{2,1,0:T(8,128)(2,1)}, u32[]{:S(2)}) copy-start(bf16[1,512,3072]{2,1,0:T(8,128)(2,1)} %all-gather.2.cloned.1.call-done) | copy-start | bytes 9437188
  366.1 1.1 copy-start.6
  366.1 250.5 %reduce-scatter.3.cloned.1.call-start = ((), (), s32[]{:S(2)}) async-start(), calls=%async_computation.5 | async-start | bytes 7864320 | tf_op jit(solution)/shard_map/reduce_scatter | solution.py:99
  374.1 306.2 %reduce-scatter.5.cloned.1.call-start = ((), (), s32[]{:S(2)}) async-start(), calls=%async_computation.6 | async-start | bytes 3932160 | tf_op jit(solution)/shard_map/reduce_scatter | solution.py:121
Sparse Core Ops, SparseCore 0:
  10.4 156.3 all-gather.1
  366.2 137.0 all-reduce.2
  505.8 110.8 reduce-scatter.2
  619.5 60.7 reduce-scatter.4
